TPU v7x, 32 devices: a whole 2x2x4 slice. The times are simulated.
32 devices in a mesh: row: 8 (over z, y), col: 4 (over x, core).
Axes of the slice: x: 2, y: 2, z: 4, core: 2. Of those that a mesh axis runs over, the one named last changes fastest.
Arguments:
- tokens: bfloat16 [384, 8192], P('row', 'col'), may hold values from -6 to 6
- weight: bfloat16 [8192, 32768], P('col', 'row'), may hold values from -0.109375 to 0.109375
- tile_rows: int32 [8, 4, 256], P('row', 'col'), may hold values from 0 to 63, as said below
- tile_cols: int32 [8, 4, 256], P('row', 'col'), may hold values from 0 to 255, as said below
- tile_count: int32 [8, 4], P('row', 'col'), may hold values from 64 to 256, as said below
- hidden_cotangent: bfloat16 [384, 32768], P('col', 'row'), may hold values from -6 to 6
Outputs:
- hidden: bfloat16 [384, 32768], P('col', 'row')
- input_grad: bfloat16 [384, 8192], P('row', 'col')
- weight_grad: bfloat16 [8192, 32768], P('col', 'row')
Inputs may be any that keep to these rules, and one draw needn't show every extreme that they name: tile_rows[r, c, k] is a row block of the weight (tiles of 128 x 128) among the 16 blocks from c * 16 on, which index c of col holds. tile_cols[r, c, k] is a column block among the 32 blocks from r * 32 on, which index r of row holds; the 256 candidate tiles of one device are distinct. The first tile_count[r, c] candidates of device (r, c) are its nonzero tiles; some device holds 256.
All inputs are finite; a program needn't handle non-finite values.
Results may differ from a plain program's by a relative error of at most 0.0049.
Values may be sent and summed in bfloat16 or wider, within the bound.
A program may use at most 128 MiB of HBM per device.

v0:
```python
import jax
import jax.numpy as jnp
from jax import lax
from jax.sharding import PartitionSpec as P

TILE = 128


def exchange_sum(partial, axis):
    n = lax.psum(1, axis)
    rows = partial.shape[0] // n
    mine = lax.all_to_all(
        partial.reshape(n, rows, partial.shape[1]), axis, split_axis=0, concat_axis=0
    )
    return mine.astype(jnp.float32).sum(axis=0)


def on_device(tokens, weight, tile_rows, tile_cols, tile_count, hidden_cotangent):
    row_index = lax.axis_index("row")
    col_index = lax.axis_index("col")
    row_blocks = weight.shape[0] // TILE
    col_blocks = weight.shape[1] // TILE
    capacity = tile_rows.shape[2]
    local_rows = tile_rows.reshape(capacity) - col_index * row_blocks
    local_cols = tile_cols.reshape(capacity) - row_index * col_blocks
    is_live = jnp.arange(capacity) < tile_count.reshape(())
    row_pick = ((local_rows[None, :] == jnp.arange(row_blocks)[:, None]) & is_live[None, :]).astype(
        jnp.bfloat16
    )
    col_pick = (local_cols[:, None] == (jnp.arange(weight.shape[1]) // TILE)[None, :]).astype(
        jnp.bfloat16
    )
    mask = jnp.dot(row_pick, col_pick, preferred_element_type=jnp.float32)
    live = (mask > 0.5)[:, None, :]
    shaped = weight.reshape(row_blocks, TILE, weight.shape[1])
    masked = jnp.where(live, shaped, jnp.zeros_like(shaped)).reshape(weight.shape)
    full_tokens = lax.all_gather(tokens, "row", axis=0, tiled=True)
    partial = jnp.dot(full_tokens, masked, preferred_element_type=jnp.float32)
    pre_act = exchange_sum(partial.astype(jnp.bfloat16), "col")
    gate_value = jax.nn.sigmoid(pre_act)
    hidden = (pre_act * gate_value).astype(jnp.bfloat16)
    silu_slope = gate_value * (1.0 + pre_act * (1.0 - gate_value))
    grad_pre = (hidden_cotangent.astype(jnp.float32) * silu_slope).astype(jnp.bfloat16)
    full_grads = lax.all_gather(grad_pre, "col", axis=0, tiled=True)
    share = lax.dot_general(
        full_grads, masked, (((1,), (1,)), ((), ())), preferred_element_type=jnp.float32
    )
    input_grad = exchange_sum(share.astype(jnp.bfloat16), "row").astype(jnp.bfloat16)
    full = lax.dot_general(
        full_tokens, full_grads, (((0,), (0,)), ((), ())), preferred_element_type=jnp.float32
    ).reshape(row_blocks, TILE, weight.shape[1])
    weight_grad = jnp.where(live, full, 0.0).astype(jnp.bfloat16).reshape(weight.shape)
    return (hidden, input_grad, weight_grad)


def solution(mesh):
    in_specs = (
        P("row", "col"),
        P("col", "row"),
        P("row", "col", None),
        P("row", "col", None),
        P("row", "col"),
        P("col", "row"),
    )
    out_specs = (P("col", "row"), P("row", "col"), P("col", "row"))
    return jax.shard_map(
        on_device, mesh=mesh, in_specs=in_specs, out_specs=out_specs, check_vma=False
    )
```

profile of v0, /device:TPU:0, one launch (start us, length us, event | category | flops | bytes accessed | tf_op | source)
XLA Modules:
  0.0 230.9 jit_solution(18191495320413865887)
XLA Ops:
  7.2 0.0 all-gather.3.cloned.1.call-start
  7.2 0.7 all-gather.3.cloned.1.call-update
  7.9 0.0 all-gather.5.cloned.1.call-start
  8.6 0.7 broadcast_subtract_fusion.1
  9.3 0.7 broadcast_subtract_fusion
  10.0 0.8 convolution_compare_fusion
  10.8 0.8 copy.9
  11.6 22.5 %copy.10 = bf16[2048,4096]{0,1:T(8,128)(2,1)} copy(bf16[2048,4096]{1,0:T(8,128)(2,1)} %param.7) | data formatting | bytes 33554432 | tf_op args[1]
  34.1 23.0 %all-gather.3.cloned.1.call-done = bf16[384,2048]{1,0:T(8,128)(2,1)} async-done(((bf16[48,2048]{1,0:T(8,128)(2,1)}), bf16[384,2048]{1,0:T(8,128)(2,1)}) %all-gather.3.cloned.1.call-update) | async-done | bytes 1572880 | tf_op jit(solution)/shard_map/all_gather | solution.py:37
  57.1 26.5 %broadcast_in_dim.29 = pred[16,128,4096]{1,0,2:T(8,128)(4,1)S(1)} broadcast(pred[16,4096]{0,1:T(8,128)(4,1)S(1)} %copy.9), dimensions={0,2} | broadcast | bytes 8454144 | tf_op jit(solution)/shard_map/jit(_where)/broadcast_in_dim | solution.py:36
  83.6 0.0 copy-start
  83.6 13.5 %fusion.5 = bf16[4096,384]{0,1:T(8,128)(2,1)S(1)} fusion(bf16[384,2048]{1,0:T(8,128)(2,1)S(1)} %copy-done.2, bf16[2048,4096]{0,1:T(8,128)(2,1)} %copy.10, pred[512,8,16,128]{3,2,1,0:T(8,128)(4,1)S(1)} %bitcast.28), kind=kOutput, calls=%fused_computation.8 | convolution fusion | flops 6452412416 | bytes 29884416 | tf_op jit(solution)/shard_map/dot_general | solution.py:38
  97.2 39.4 %all_to_all.10 = bf16[4,96,4096]{2,1,0:T(8,128)(2,1)S(1)} all-to-all(bf16[4,96,4096]{2,1,0:T(8,128)(2,1)S(1)} %bitcast.31), channel_id=1, replica_groups=mesh['row'=8,'col'=4] {'col'}, dimensions={0} | all-to-all | bytes 6291456 | tf_op jit(solution)/shard_map/all_to_all | solution.py:12
  136.6 0.5 convert_reduce_fusion
  137.1 0.6 copy-done.1
  137.8 1.8 multiply_convert_fusion
  139.6 0.0 all-gather.5.cloned.1.call-update
  139.6 26.1 %all-gather.5.cloned.1.call-done = bf16[384,4096]{1,0:T(8,128)(2,1)} async-done(((bf16[96,4096]{1,0:T(8,128)(2,1)}), bf16[384,4096]{1,0:T(8,128)(2,1)}) %all-gather.5.cloned.1.call-update) | async-done | bytes 3145744 | tf_op jit(solution)/shard_map/all_gather | solution.py:44
  165.7 13.5 %fusion.7 = bf16[384,2048]{1,0:T(8,128)(2,1)} fusion(bf16[384,4096]{1,0:T(8,128)(2,1)} %all-gather.5.cloned.1.call-done, bf16[2048,4096]{0,1:T(8,128)(2,1)} %copy.10, pred[512,8,16,128]{3,2,1,0:T(8,128)(4,1)} %bitcast.29), kind=kOutput, calls=%fused_computation.11 | convolution fusion | flops 6451625984 | bytes 29884416 | tf_op jit(solution)/shard_map/dot_general | solution.py:45
  179.2 5.5 %all-to-all-start.1 = ((bf16[8,48,2048]{2,1,0:T(8,128)(2,1)}), bf16[8,48,2048]{2,1,0:T(8,128)(2,1)S(1)}, u32[]{:S(2)}, u32[]{:S(2)}) async-start(bf16[8,48,2048]{2,1,0:T(8,128)(2,1)} %bitcast.5), calls=%async_computation.1 | async-start | bytes 3145728 | tf_op jit(solution)/shard_map/all_to_all | solution.py:12
  184.7 17.3 %fusion = bf16[2048,4096]{0,1:T(8,128)(2,1)} fusion(pred[512,8,16,128]{3,2,1,0:T(8,128)(4,1)} %bitcast.30, bf16[384,4096]{1,0:T(8,128)(2,1)} %all-gather.5.cloned.1.call-done, bf16[384,2048]{1,0:T(8,128)(2,1)S(1)} %copy-done.2), kind=kOutput, calls=%fused_computation.1 | convolution fusion | flops 6459228160 | bytes 29884416 | tf_op jit(solution)/shard_map/dot_general | solution.py:49
  201.9 21.2 %copy.11 = bf16[2048,4096]{1,0:T(8,128)(2,1)} copy(bf16[2048,4096]{0,1:T(8,128)(2,1)} %fusion) | data formatting | bytes 33554432
  223.1 0.0 all-to-all-done.1
  223.1 0.9 reduce_sum.22
  (6 shorter events, 0.0 us)
Async XLA Ops:
  7.2 49.9 %all-gather.3.cloned.1.call-start = ((), (), s32[]{:S(2)}) async-start(), calls=%async_computation.2 | async-start | bytes 1769472 | tf_op jit(solution)/shard_map/all_gather | solution.py:37
  7.9 157.8 %all-gather.5.cloned.1.call-start = ((), (), s32[]{:S(2)}) async-start(), calls=%async_computation.3 | async-start | bytes 3932160 | tf_op jit(solution)/shard_map/all_gather | solution.py:44
  57.1 26.5 %copy-start.2 = (bf16[384,2048]{1,0:T(8,128)(2,1)S(1)}, bf16[384,2048]{1,0:T(8,128)(2,1)}, u32[]{:S(2)}) copy-start(bf16[384,2048]{1,0:T(8,128)(2,1)} %all-gather.3.cloned.1.call-done) | copy-start | bytes 4718596
  83.6 13.6 %copy-start = (pred[16,128,4096]{1,0,2:T(8,128)(4,1)}, pred[16,128,4096]{1,0,2:T(8,128)(4,1)S(1)}, u32[]{:S(2)}) copy-start(pred[16,128,4096]{1,0,2:T(8,128)(4,1)S(1)} %broadcast_in_dim.29) | copy-start | bytes 25165828
  136.6 1.1 copy-start.1
  179.2 44.0 %all-to-all-start.1 = ((bf16[8,48,2048]{2,1,0:T(8,128)(2,1)}), bf16[8,48,2048]{2,1,0:T(8,128)(2,1)S(1)}, u32[]{:S(2)}, u32[]{:S(2)}) async-start(bf16[8,48,2048]{2,1,0:T(8,128)(2,1)} %bitcast.5), calls=%async_computation.1 | async-start | bytes 3145728 | tf_op jit(solution)/shard_map/all_to_all | solution.py:12
Sparse Core Ops, SparseCore 0:
  10.2 46.8 all-gather.2
  139.7 25.9 all-gather.4
where the time goes:
time: 232 us; the launch traced here: 231 us
  local copies, waits for them, and re-layouts  71.6 us (31%)
  waiting for transfers between devices  49.8 us (21%)
  matrix products  45 us (19%)
  blocking collectives  39.4 us (17%)
  between operations  14.8 us (6%)
  starting transfers between devices  5.59 us (2%)
  other arithmetic  4.66 us (2%)
    unnamed x8, local copies, waits for them, and re-layouts  44.3 us
    all_to_all x1, blocking collectives, exchange_sum(): lax.all_to_all(partial.reshape(n, rows, partial.shape[1]), axis, split_ax...  39.4 us
    broadcast_in_dim x1, local copies, waits for them, and re-layouts, on_device(): jnp.where(live, shaped, jnp.zeros_like(shaped)).reshape(weight.shape)  26.5 us
    all_gather x1, waiting for transfers between devices, on_device(): full_grads = lax.all_gather(grad_pre, 'col', axis=0, tiled=True)  26.1 us
    all_gather x1, waiting for transfers between devices, on_device(): full_tokens = lax.all_gather(tokens, 'row', axis=0, tiled=True)  23 us
    dot_general x1, matrix products, on_device(): lax.dot_general(full_tokens, full_grads, (((0,), (0,)), ((), ())), prefer...  17.3 us
    dot_general x1, matrix products, on_device(): partial = jnp.dot(full_tokens, masked, preferred_element_type=jnp.float32)  13.5 us
    dot_general x1, matrix products, on_device(): lax.dot_general(full_grads, masked, (((1,), (1,)), ((), ())), preferred_e...  13.5 us
  transfers between devices with their start and end apart: 3, of which 2 were waited for; matrix products, arithmetic and copies ran while one was open for 28% of the time, Pallas kernels for 0%

commit v1 on v0

--- a/solution.py
+++ b/solution.py
@@ -41,7 +41,12 @@
     hidden = (pre_act * gate_value).astype(jnp.bfloat16)
     silu_slope = gate_value * (1.0 + pre_act * (1.0 - gate_value))
     grad_pre = (hidden_cotangent.astype(jnp.float32) * silu_slope).astype(jnp.bfloat16)
-    full_grads = lax.all_gather(grad_pre, "col", axis=0, tiled=True)
+    ring = [grad_pre]
+    for hop in range(3):
+        ring.append(lax.ppermute(ring[-1], "col", [(dev, (dev + 1) % 4) for dev in range(4)]))
+    full_grads = jnp.roll(
+        jnp.concatenate(ring[::-1], axis=0), (lax.axis_index("col") + 1) * ring[0].shape[0], axis=0
+    )
     share = lax.dot_general(
         full_grads, masked, (((1,), (1,)), ((), ())), preferred_element_type=jnp.float32
     )

time: 232 us -> 241 us (1.039)
  waiting for transfers between devices: 49.8 us -> 58 us
  matrix products: 45 us -> 47.9 us
    ppermute x0 -> x3, waiting for transfers between devices: none -> 34.2 us  [on_device(): lax.ppermute(ring[-1], 'col', [(dev, (dev + 1) % 4) for dev in range(4)])]
    all_gather x1 -> x0, waiting for transfers between devices: 26.1 us -> none  [on_device(): full_grads = lax.all_gather(grad_pre, 'col', axis=0, tiled=True)]
    unnamed x8 -> x19, local copies, waits for them, and re-layouts: 44.3 us -> 44.1 us
  transfers between devices with their start and end apart: 3 -> 5, of which waited for: 2 -> 4; matrix products, arithmetic and copies ran while one was open for 28% -> 27% of each run, Pallas kernels for 0% -> 0%
where the time goes in v1:
time: 241 us; the launch traced here: 240 us
  local copies, waits for them, and re-layouts  71.4 us (30%)
  waiting for transfers between devices  58 us (24%)
  matrix products  47.9 us (20%)
  blocking collectives  39.6 us (16%)
  between operations  14.9 us (6%)
  other arithmetic  4.39 us (2%)
  starting transfers between devices  3.63 us (2%)
    unnamed x19, local copies, waits for them, and re-layouts  44.1 us
    all_to_all x1, blocking collectives, exchange_sum(): lax.all_to_all(partial.reshape(n, rows, partial.shape[1]), axis, split_ax...  39.6 us
    ppermute x3, waiting for transfers between devices, on_device(): lax.ppermute(ring[-1], 'col', [(dev, (dev + 1) % 4) for dev in range(4)])  34.2 us
    broadcast_in_dim x1, local copies, waits for them, and re-layouts, on_device(): jnp.where(live, shaped, jnp.zeros_like(shaped)).reshape(weight.shape)  26.5 us
    all_gather x1, waiting for transfers between devices, on_device(): full_tokens = lax.all_gather(tokens, 'row', axis=0, tiled=True)  23 us
    dot_general x1, matrix products, on_device(): lax.dot_general(full_tokens, full_grads, (((0,), (0,)), ((), ())), prefer...  18.1 us
    dot_general x1, matrix products, on_device(): lax.dot_general(full_grads, masked, (((1,), (1,)), ((), ())), preferred_e...  15.5 us
    dot_general x1, matrix products, on_device(): partial = jnp.dot(full_tokens, masked, preferred_element_type=jnp.float32)  13.5 us
  transfers between devices with their start and end apart: 5, of which 4 were waited for; matrix products, arithmetic and copies ran while one was open for 27% of the time, Pallas kernels for 0%

profile of v1, /device:TPU:0, one launch (start us, length us, event | category | flops | bytes accessed | tf_op | source)
XLA Modules:
  0.0 239.8 jit_solution(18035669964082318997)
XLA Ops:
  7.2 0.7 all-gather.2.cloned.1.call-update
  8.6 0.7 broadcast_subtract_fusion.1
  9.3 0.7 broadcast_subtract_fusion
  9.9 0.8 convolution_compare_fusion
  10.8 0.8 copy.9
  11.6 22.5 %copy.10 = bf16[2048,4096]{0,1:T(8,128)(2,1)} copy(bf16[2048,4096]{1,0:T(8,128)(2,1)} %param.7) | data formatting | bytes 33554432 | tf_op args[1]
  34.1 23.0 %all-gather.2.cloned.1.call-done = bf16[384,2048]{1,0:T(8,128)(2,1)} async-done(((bf16[48,2048]{1,0:T(8,128)(2,1)}), bf16[384,2048]{1,0:T(8,128)(2,1)}) %all-gather.2.cloned.1.call-update) | async-done | bytes 1572880 | tf_op jit(solution)/shard_map/all_gather | solution.py:37
  57.1 26.5 %broadcast_in_dim.29 = pred[16,128,4096]{1,0,2:T(8,128)(4,1)S(1)} broadcast(pred[16,4096]{0,1:T(8,128)(4,1)S(1)} %copy.9), dimensions={0,2} | broadcast | bytes 8454144 | tf_op jit(solution)/shard_map/jit(_where)/broadcast_in_dim | solution.py:36
  83.6 13.5 %fusion.5 = bf16[4096,384]{0,1:T(8,128)(2,1)S(1)} fusion(bf16[384,2048]{1,0:T(8,128)(2,1)S(1)} %copy-done.3, bf16[2048,4096]{0,1:T(8,128)(2,1)} %copy.10, pred[512,8,16,128]{3,2,1,0:T(8,128)(4,1)S(1)} %bitcast.26), kind=kOutput, calls=%fused_computation.8 | convolution fusion | flops 6452412416 | bytes 29884416 | tf_op jit(solution)/shard_map/dot_general | solution.py:38
  97.2 39.6 %all_to_all.10 = bf16[4,96,4096]{2,1,0:T(8,128)(2,1)S(1)} all-to-all(bf16[4,96,4096]{2,1,0:T(8,128)(2,1)S(1)} %bitcast.29), channel_id=1, replica_groups=mesh['row'=8,'col'=4] {'col'}, dimensions={0} | all-to-all | bytes 6291456 | tf_op jit(solution)/shard_map/all_to_all | solution.py:12
  136.8 0.5 convert_reduce_fusion
  137.3 1.5 multiply_convert_fusion
  138.8 11.4 %collective-permute-done = bf16[96,4096]{1,0:T(8,128)(2,1)S(1)} collective-permute-done((bf16[96,4096]{1,0:T(8,128)(2,1)S(1)}, bf16[96,4096]{1,0:T(8,128)(2,1)S(1)}, u32[]{:S(2)}, u32[]{:S(2)}) %collective-permute-start) | collective-permute-done | bytes 786464 | tf_op jit(solution)/shard_map/ppermute | solution.py:46
  150.3 11.4 %collective-permute-done.1 = bf16[96,4096]{1,0:T(8,128)(2,1)S(1)} collective-permute-done((bf16[96,4096]{1,0:T(8,128)(2,1)S(1)}, bf16[96,4096]{1,0:T(8,128)(2,1)S(1)}, u32[]{:S(2)}, u32[]{:S(2)}) %collective-permute-start.1) | collective-permute-done | bytes 786464 | tf_op jit(solution)/shard_map/ppermute | solution.py:46
  161.7 11.4 %collective-permute-done.2 = bf16[96,4096]{1,0:T(8,128)(2,1)S(1)} collective-permute-done((bf16[96,4096]{1,0:T(8,128)(2,1)S(1)}, bf16[96,4096]{1,0:T(8,128)(2,1)S(1)}, u32[]{:S(2)}, u32[]{:S(2)}) %collective-permute-start.2) | collective-permute-done | bytes 786464 | tf_op jit(solution)/shard_map/ppermute | solution.py:46
  173.2 0.1 constant_dynamic-update-slice_fusion.6
  173.2 0.1 constant_dynamic-update-slice_fusion.5
  173.3 0.1 constant_dynamic-update-slice_fusion.4
  173.4 0.1 constant_dynamic-update-slice_fusion.2
  173.6 15.5 %fusion.7 = bf16[384,2048]{1,0:T(8,128)(2,1)} fusion(bf16[2048,4096]{0,1:T(8,128)(2,1)} %copy.10, pred[512,8,16,128]{3,2,1,0:T(8,128)(4,1)} %bitcast.27, bf16[768,4096]{1,0:T(8,128)(2,1)S(1)} %constant_dynamic-update-slice_fusion, s32[]{:T(128)S(6)} %select_n.35), kind=kOutput, calls=%fused_computation.11 | convolution fusion | flops 6451625984 | bytes 29884420 | tf_op jit(solution)/shard_map/dot_general | solution.py:50
  189.1 3.6 %all-to-all-start.1 = ((bf16[8,48,2048]{2,1,0:T(8,128)(2,1)}), bf16[8,48,2048]{2,1,0:T(8,128)(2,1)S(1)}, u32[]{:S(2)}, u32[]{:S(2)}) async-start(bf16[8,48,2048]{2,1,0:T(8,128)(2,1)} %bitcast.5), calls=%async_computation.1 | async-start | bytes 3145728 | tf_op jit(solution)/shard_map/all_to_all | solution.py:12
  192.7 18.1 %fusion = bf16[2048,4096]{0,1:T(8,128)(2,1)} fusion(pred[512,8,16,128]{3,2,1,0:T(8,128)(4,1)} %bitcast.28, bf16[384,2048]{1,0:T(8,128)(2,1)S(1)} %copy-done.4, bf16[768,4096]{1,0:T(8,128)(2,1)} %copy-done.2, s32[]{:T(128)S(6)} %select_n.35), kind=kOutput, calls=%fused_computation.1 | convolution fusion | flops 6459228160 | bytes 29884420 | tf_op jit(solution)/shard_map/dot_general | solution.py:54
  210.8 21.2 %copy.11 = bf16[2048,4096]{1,0:T(8,128)(2,1)} copy(bf16[2048,4096]{0,1:T(8,128)(2,1)} %fusion) | data formatting | bytes 33554432
  232.0 0.9 reduce_sum.22
  (21 shorter events, 0.3 us)
Async XLA Ops:
  7.2 49.9 %all-gather.2.cloned.1.call-start = ((), (), s32[]{:S(2)}) async-start(), calls=%async_computation.2 | async-start | bytes 1769472 | tf_op jit(solution)/shard_map/all_gather | solution.py:37
  57.1 26.5 %copy-start.3 = (bf16[384,2048]{1,0:T(8,128)(2,1)S(1)}, bf16[384,2048]{1,0:T(8,128)(2,1)}, u32[]{:S(2)}) copy-start(bf16[384,2048]{1,0:T(8,128)(2,1)} %all-gather.2.cloned.1.call-done) | copy-start | bytes 4718596
  83.6 13.6 %copy-start = (pred[16,128,4096]{1,0,2:T(8,128)(4,1)}, pred[16,128,4096]{1,0,2:T(8,128)(4,1)S(1)}, u32[]{:S(2)}) copy-start(pred[16,128,4096]{1,0,2:T(8,128)(4,1)S(1)} %broadcast_in_dim.29) | copy-start | bytes 25165828
  97.2 40.1 %copy-start.1 = (bf16[96,4096]{1,0:T(8,128)(2,1)S(1)}, bf16[96,4096]{1,0:T(8,128)(2,1)}, u32[]{:S(2)}) copy-start(bf16[96,4096]{1,0:T(8,128)(2,1)} %param.11) | copy-start | bytes 2359300
  138.8 11.4 %collective-permute-start = (bf16[96,4096]{1,0:T(8,128)(2,1)S(1)}, bf16[96,4096]{1,0:T(8,128)(2,1)S(1)}, u32[]{:S(2)}, u32[]{:S(2)}) collective-permute-start(bf16[96,4096]{1,0:T(8,128)(2,1)S(1)} %get-tuple-element.6), channel_id=1, source_target_pairs={{0,1},{1,2},{2,3},{3,0},{4,5},{5,6},{6,7},{7,4},{8,9},{9,10},{10,1... | collective-permute-start | bytes 2359304 | tf_op jit(solution)/shard_map/ppermute | solution.py:46
  150.3 11.4 %collective-permute-start.1 = (bf16[96,4096]{1,0:T(8,128)(2,1)S(1)}, bf16[96,4096]{1,0:T(8,128)(2,1)S(1)}, u32[]{:S(2)}, u32[]{:S(2)}) collective-permute-start(bf16[96,4096]{1,0:T(8,128)(2,1)S(1)} %collective-permute-done), channel_id=1, source_target_pairs={{0,1},{1,2},{2,3},{3,0},{4,5},{5,6},{6,7},{7,4},{8,9},{9,10},{10,1... | collective-permute-start | bytes 2359304 | tf_op jit(solution)/shard_map/ppermute | solution.py:46
  161.7 11.4 %collective-permute-start.2 = (bf16[96,4096]{1,0:T(8,128)(2,1)S(1)}, bf16[96,4096]{1,0:T(8,128)(2,1)S(1)}, u32[]{:S(2)}, u32[]{:S(2)}) collective-permute-start(bf16[96,4096]{1,0:T(8,128)(2,1)S(1)} %collective-permute-done.1), channel_id=1, source_target_pairs={{0,1},{1,2},{2,3},{3,0},{4,5},{5,6},{6,7},{7,4},{8,9},{9,10},{10,1... | collective-permute-start | bytes 2359304 | tf_op jit(solution)/shard_map/ppermute | solution.py:46
  173.6 15.5 %copy-start.2 = (bf16[768,4096]{1,0:T(8,128)(2,1)}, bf16[768,4096]{1,0:T(8,128)(2,1)S(1)}, u32[]{:S(2)}) copy-start(bf16[768,4096]{1,0:T(8,128)(2,1)S(1)} %constant_dynamic-update-slice_fusion) | copy-start | bytes 18874372
  173.6 19.1 %copy-start.4 = (bf16[384,2048]{1,0:T(8,128)(2,1)S(1)}, bf16[384,2048]{1,0:T(8,128)(2,1)}, u32[]{:S(2)}) copy-start(bf16[384,2048]{1,0:T(8,128)(2,1)} %all-gather.2.cloned.1.call-done) | copy-start | bytes 4718596
  189.1 42.9 %all-to-all-start.1 = ((bf16[8,48,2048]{2,1,0:T(8,128)(2,1)}), bf16[8,48,2048]{2,1,0:T(8,128)(2,1)S(1)}, u32[]{:S(2)}, u32[]{:S(2)}) async-start(bf16[8,48,2048]{2,1,0:T(8,128)(2,1)} %bitcast.5), calls=%async_computation.1 | async-start | bytes 3145728 | tf_op jit(solution)/shard_map/all_to_all | solution.py:12
Sparse Core Ops, SparseCore 0:
  10.2 46.8 all-gather.1
